TPU v7x, 32 devices: a whole 2x2x4 slice. The times are simulated.
32 devices in a mesh: row: 4 (over z), col: 8 (over y, x, core).
Axes of the slice: x: 2, y: 2, z: 4, core: 2. Of those that a mesh axis runs over, the one named last changes fastest.
Arguments:
- weight: float32 [16384, 16384], P('row', 'col'), may hold values from -0.046875 to 0.046875
- leak: float32 [16384], P('col'), may hold values from 0.1 to 1
- rates: float32 [3, 256, 16384], P(None, 'row', 'col'), may hold values from -0.95 to 0.95
- cotangent: float32 [256, 16384], P('row', 'col'), may hold values from -2 to 2
Outputs:
- grad_input: float32 [256, 16384], P('row', 'col')
- grad_weight: float32 [16384, 16384], P('row', 'col')
- grad_noise: float32 [3, 16384], P(None, 'row')
All inputs are finite; a program needn't handle non-finite values.
Results may differ from a plain program's by a relative error of at most 0.0001.
Values sent between devices are 32-bit elements; how exact they have to be, the bound alone decides.
A program may use at most 192 MiB of HBM per device.

v0:
```python
import jax
import jax.numpy as jnp
from jax import lax
from jax.sharding import PartitionSpec as P

TSTEPS = 3


def shards(weight, leak, rates, cotangent):
    n_col = lax.axis_size("col")
    own_rows = cotangent.shape[0]
    local_units = cotangent.shape[1]
    full_rates = lax.all_gather(rates, "row", axis=1, tiled=True)
    grad_weight = jnp.zeros(weight.shape, jnp.float32)
    noise_list = []
    carried = cotangent
    for step_back in range(TSTEPS - 1, -1, -1):
        scaled = leak[None, :] * carried
        spread = scaled.reshape(own_rows, local_units // n_col, n_col)
        by_col = lax.all_to_all(spread, "col", split_axis=2, concat_axis=1, tiled=True)
        by_row = lax.all_to_all(by_col, "row", split_axis=1, concat_axis=0, tiled=True)
        gathered = lax.all_gather(by_row, "col", axis=2, tiled=True)
        unit_block = gathered.reshape(gathered.shape[0], gathered.shape[1] * gathered.shape[2])
        rates_now = full_rates[step_back]
        noise_list.insert(0, jnp.sum(unit_block, axis=0))
        grad_weight = grad_weight + lax.dot_general(
            unit_block,
            rates_now,
            (((0,), (0,)), ((), ())),
            precision=lax.Precision.HIGHEST,
            preferred_element_type=jnp.float32,
        )
        partial_sum = jnp.dot(
            unit_block, weight, precision=lax.Precision.HIGHEST, preferred_element_type=jnp.float32
        )
        adjoint = lax.psum_scatter(partial_sum, "row", scatter_dimension=0, tiled=True)
        local_rates = rates[step_back]
        carried = (1.0 - leak[None, :]) * carried + (1.0 - local_rates * local_rates) * adjoint
    return (carried, grad_weight, jnp.stack(noise_list))


def solution(mesh):
    placed = (P("row", "col"), P("col"), P(None, "row", "col"), P("row", "col"))
    return jax.shard_map(
        shards,
        mesh=mesh,
        in_specs=placed,
        out_specs=(P("row", "col"), P("row", "col"), P(None, "row")),
        check_vma=False,
    )
```

profile of v0, /device:TPU:0, one launch (start us, length us, event | category | flops | bytes accessed | tf_op | source)
XLA Modules:
  0.0 634.5 jit_solution(5892808969612367369)
XLA Ops:
  7.2 1.1 broadcast_multiply_fusion.2
  8.6 0.4 copy.20
  9.0 14.7 %all_to_all.108 = f32[64,256,8]{1,0,2:T(8,128)S(1)} all-to-all(f32[64,256,8]{1,0,2:T(8,128)S(1)} %copy.20), channel_id=1, replica_groups=mesh['row'=4,'col'=8] {'col'}, dimensions={2} | all-to-all | bytes 1048576 | tf_op jit(solution)/shard_map/all_to_all | solution.py:20
  24.1 0.5 broadcast.24
  24.6 9.3 %reduce.3 = f32[2048,64]{1,0:T(8,128)S(1)} reduce(f32[2048,1,64]{2,1,0:T(1,128)S(1)} %bitcast.75, f32[]{:T(128)} %broadcast.24), dimensions={1}, to_apply=%bitcast.64.reduce_sub_computation | reduce | bytes 1048580
  33.9 0.7 reshape.48
  34.6 18.6 %all_to_all.109 = f32[4,1,32768]{2,1,0:T(1,128)S(1)} all-to-all(f32[4,1,32768]{2,1,0:T(1,128)S(1)} %reshape.48), channel_id=1, replica_groups=mesh['row'=4,'col'=8] {'row'}, dimensions={0} | all-to-all | bytes 1048576 | tf_op jit(solution)/shard_map/all_to_all | solution.py:21
  53.2 2.1 reduce.4
  55.3 1.3 reshape.49
  57.0 1.0 copy.24
  58.3 34.2 %all-gather.5.cloned.1.call-done = f32[256,512,8]{1,0,2:T(8,128)} async-done(((f32[256,512,1]{1,0,2:T(8,128)}), f32[256,512,8]{1,0,2:T(8,128)}) %all-gather.5.cloned.1.call-update) | async-done | bytes 4194320 | tf_op jit(solution)/shard_map/all_gather | solution.py:22
  92.6 5.4 copy.25
  98.0 33.9 %fusion.9 = f32[256,2048]{1,0:T(8,128)} fusion(f32[4096,2048]{1,0:T(8,128)} %param.4, f32[256,512,8]{0,2,1:T(8,128)} %copy.25), kind=kOutput, calls=%fused_computation.10 | convolution fusion | flops 25769803776 | bytes 39845888 | tf_op jit(solution)/shard_map/dot_general | solution.py:33
  132.0 43.7 %reduce-scatter.4.cloned.1.call-done = f32[64,2048]{1,0:T(8,128)} async-done(((f32[256,2048]{1,0:T(8,128)}), f32[64,2048]{1,0:T(8,128)}) %reduce-scatter.4.cloned.1.call-update) | async-done | bytes 524304 | tf_op jit(solution)/shard_map/reduce_scatter | solution.py:36
  175.7 1.3 broadcast_multiply_fusion.1
  177.7 13.7 %all_to_all.110 = f32[64,256,8]{1,0,2:T(8,128)S(1)} all-to-all(f32[64,256,8]{1,0,2:T(8,128)S(1)} %copy.27), channel_id=1, replica_groups=mesh['row'=4,'col'=8] {'col'}, dimensions={2} | all-to-all | bytes 1048576 | tf_op jit(solution)/shard_map/all_to_all | solution.py:20
  191.8 9.3 %reduce.5 = f32[2048,64]{1,0:T(8,128)S(1)} reduce(f32[2048,1,64]{2,1,0:T(1,128)S(1)} %bitcast.76, f32[]{:T(128)} %broadcast.24), dimensions={1}, to_apply=%bitcast.66.reduce_sub_computation | reduce | bytes 1048580
  201.1 0.7 reshape.50
  201.8 16.6 %all_to_all.111 = f32[4,1,32768]{2,1,0:T(1,128)S(1)} all-to-all(f32[4,1,32768]{2,1,0:T(1,128)S(1)} %reshape.50), channel_id=1, replica_groups=mesh['row'=4,'col'=8] {'row'}, dimensions={0} | all-to-all | bytes 1048576 | tf_op jit(solution)/shard_map/all_to_all | solution.py:21
  218.4 2.1 reduce.6
  220.5 1.3 reshape.51
  222.2 1.0 copy.31
  223.4 34.3 %all-gather.7.cloned.1.call-done = f32[256,512,8]{1,0,2:T(8,128)} async-done(((f32[256,512,1]{1,0,2:T(8,128)}), f32[256,512,8]{1,0,2:T(8,128)}) %all-gather.7.cloned.1.call-update) | async-done | bytes 4194320 | tf_op jit(solution)/shard_map/all_gather | solution.py:22
  257.7 5.5 copy.32
  263.2 33.8 %fusion.5 = f32[256,2048]{1,0:T(8,128)} fusion(f32[4096,2048]{1,0:T(8,128)} %param.4, f32[256,512,8]{0,2,1:T(8,128)} %copy.32), kind=kOutput, calls=%fused_computation.6 | convolution fusion | flops 25769803776 | bytes 39845888 | tf_op jit(solution)/shard_map/dot_general | solution.py:33
  297.2 0.5 all-gather.11.cloned.1.call-update
  297.8 43.2 %reduce-scatter.6.cloned.1.call-done = f32[64,2048]{1,0:T(8,128)} async-done(((f32[256,2048]{1,0:T(8,128)}), f32[64,2048]{1,0:T(8,128)}) %reduce-scatter.6.cloned.1.call-update) | async-done | bytes 524304 | tf_op jit(solution)/shard_map/reduce_scatter | solution.py:36
  340.9 2.0 broadcast_multiply_fusion
  343.3 0.4 copy.34
  343.7 13.5 %all_to_all.112 = f32[64,256,8]{1,0,2:T(8,128)} all-to-all(f32[64,256,8]{1,0,2:T(8,128)S(1)} %copy.34), channel_id=1, replica_groups=mesh['row'=4,'col'=8] {'col'}, dimensions={2} | all-to-all | bytes 1048576 | tf_op jit(solution)/shard_map/all_to_all | solution.py:20
  357.2 1.4 copy.47
  358.5 10.3 %reduce.7 = f32[2048,64]{1,0:T(8,128)} reduce(f32[2048,1,64]{2,1,0:T(1,128)S(1)} %bitcast.77, f32[]{:T(128)} %broadcast.24), dimensions={1}, to_apply=%bitcast.68.reduce_sub_computation | reduce | bytes 1048580
  368.9 1.9 reshape.52
  370.7 32.0 %all_to_all.113 = f32[4,1,32768]{2,1,0:T(1,128)S(1)} all-to-all(f32[4,1,32768]{2,1,0:T(1,128)S(1)} %reshape.52), channel_id=1, replica_groups=mesh['row'=4,'col'=8] {'row'}, dimensions={0} | all-to-all | bytes 1048576 | tf_op jit(solution)/shard_map/all_to_all | solution.py:21
  402.7 2.1 reduce.8
  404.8 1.3 reshape.53
  406.5 1.0 copy.38
  407.8 2.6 reduce_sum.29
  410.7 57.2 %all-gather.11.cloned.1.call-done = f32[3,256,2048]{2,1,0:T(8,128)} async-done(((f32[3,64,2048]{2,1,0:T(8,128)}), f32[3,256,2048]{2,1,0:T(8,128)}) %all-gather.11.cloned.1.call-update) | async-done | bytes 6291472 | tf_op jit(solution)/shard_map/all_gather | solution.py:13
  468.0 32.4 %fusion.7 = f32[4096,2048]{1,0:T(8,128)} fusion(f32[256,512,8]{0,2,1:T(8,128)} %copy.25, f32[3,256,2048]{2,1,0:T(8,128)} %all-gather.11.cloned.1.call-done), kind=kOutput, calls=%fused_computation.8 | convolution fusion | flops 25769803776 | bytes 39845888 | tf_op jit(solution)/shard_map/dot_general | solution.py:26
  500.4 2.7 reduce_sum.28
  503.4 32.7 %fusion.3 = f32[4096,2048]{1,0:T(8,128)} fusion(f32[256,512,8]{0,2,1:T(8,128)} %copy.32, f32[3,256,2048]{2,1,0:T(8,128)} %all-gather.11.cloned.1.call-done), kind=kOutput, calls=%fused_computation.4 | convolution fusion | flops 25769803776 | bytes 39845888 | tf_op jit(solution)/shard_map/dot_general | solution.py:26
  536.0 2.6 reduce_sum.27
  539.0 5.5 copy.39
  544.4 33.9 %fusion.1 = f32[256,2048]{1,0:T(8,128)} fusion(f32[4096,2048]{1,0:T(8,128)} %param.4, f32[256,512,8]{0,2,1:T(8,128)} %copy.39), kind=kOutput, calls=%fused_computation.2 | convolution fusion | flops 25769803776 | bytes 39845888 | tf_op jit(solution)/shard_map/dot_general | solution.py:33
  578.4 0.7 pad_maximum_fusion
  579.1 46.4 %add_add_fusion = f32[4096,2048]{1,0:T(8,128)} fusion(f32[4096,2048]{1,0:T(8,128)} %fusion.7, f32[4096,2048]{1,0:T(8,128)} %fusion.3, f32[256,512,8]{0,2,1:T(8,128)} %copy.39, f32[3,256,2048]{2,1,0:T(8,128)} %all-gather.11.cloned.1.call-done), kind=kOutput, calls=%fused_computation | convolution fusion | flops 25786580992 | bytes 106954752 | tf_op jit(solution)/shard_map/dot_general | solution.py:26
  625.4 1.9 fusion.11
  (41 shorter events, 5.1 us)
Async XLA Ops:
  7.2 85.4 %all-gather.5.cloned.1.call-start = ((), (), s32[]{:S(2)}) async-start(), calls=%async_computation.9 | async-start | bytes 4718592 | tf_op jit(solution)/shard_map/all_gather | solution.py:22
  58.0 117.7 %reduce-scatter.4.cloned.1.call-start = ((), (), s32[]{:S(2)}) async-start(), calls=%async_computation.10 | async-start | bytes 2621440 | tf_op jit(solution)/shard_map/reduce_scatter | solution.py:36
  98.0 33.9 %copy-start.4 = (f32[2048]{0:T(1024)S(1)}, f32[2048]{0:T(1024)}, u32[]{:S(2)}) copy-start(f32[2048]{0:T(1024)} %param.5) | copy-start | bytes 24580
  98.0 77.7 %copy-start.1 = (f32[64,2048]{1,0:T(8,128)S(1)}, f32[64,2048]{1,0:T(8,128)}, u32[]{:S(2)}) copy-start(f32[64,2048]{1,0:T(8,128)} %param.7) | copy-start | bytes 1572868
  131.9 125.9 %all-gather.7.cloned.1.call-start = ((), (), s32[]{:S(2)}) async-start(), calls=%async_computation.11 | async-start | bytes 4718592 | tf_op jit(solution)/shard_map/all_gather | solution.py:22
  223.2 117.7 %reduce-scatter.6.cloned.1.call-start = ((), (), s32[]{:S(2)}) async-start(), calls=%async_computation.12 | async-start | bytes 2621440 | tf_op jit(solution)/shard_map/reduce_scatter | solution.py:36
  263.2 77.7 %copy-start.3 = (f32[64,2048]{1,0:T(8,128)S(1)}, f32[64,2048]{1,0:T(8,128)}, u32[]{:S(2)}) copy-start(f32[64,2048]{1,0:T(8,128)} %reduce-scatter.4.cloned.1.call-done) | copy-start | bytes 1572868
  297.1 43.8 %copy-start = (f32[3,64,2048]{2,1,0:T(8,128)S(1)}, f32[3,64,2048]{2,1,0:T(8,128)}, u32[]{:S(2)}) copy-start(f32[3,64,2048]{2,1,0:T(8,128)} %param.6) | copy-start | bytes 4718596
  297.1 170.9 %all-gather.11.cloned.1.call-start = ((), (), s32[]{:S(2)}) async-start(), calls=%async_computation.15 | async-start | bytes 7864320 | tf_op jit(solution)/shard_map/all_gather | solution.py:13
  297.7 238.3 %all-gather.9.cloned.1.call-start = ((), (), s32[]{:S(2)}) async-start(), calls=%async_computation.13 | async-start | bytes 4718592 | tf_op jit(solution)/shard_map/all_gather | solution.py:22
  407.5 217.9 %reduce-scatter.8.cloned.1.call-start = ((), (), s32[]{:S(2)}) async-start(), calls=%async_computation.14 | async-start | bytes 2621440 | tf_op jit(solution)/shard_map/reduce_scatter | solution.py:36
  579.1 46.4 %copy-start.2 = (f32[64,2048]{1,0:T(8,128)S(1)}, f32[64,2048]{1,0:T(8,128)}, u32[]{:S(2)}) copy-start(f32[64,2048]{1,0:T(8,128)} %get-tuple-element.4) | copy-start | bytes 1572868
Sparse Core Ops, SparseCore 0:
  58.1 34.4 all-gather.4
  132.0 43.6 reduce-scatter.3
  223.3 34.4 all-gather.6
  297.2 43.6 reduce-scatter.5
  342.3 125.6 all-gather.10
  469.7 34.7 all-gather.8
  578.5 41.7 reduce-scatter.7
where the time goes:
time: 642 us; the launch traced here: 634 us
  waiting for transfers between devices  213 us (33%)
  matrix products  213 us (33%)
  blocking collectives  109 us (17%)
  other arithmetic  50.4 us (8%)
  local copies, waits for them, and re-layouts  33 us (5%)
  between operations  14.6 us (2%)
    dot_general x3, matrix products, shards(): lax.dot_general(unit_block, rates_now, (((0,), (0,)), ((), ())), precisio...  111 us
    dot_general x3, matrix products, shards(): jnp.dot(unit_block, weight, precision=lax.Precision.HIGHEST, preferred_el...  102 us
    reduce_scatter x3, waiting for transfers between devices, shards(): lax.psum_scatter(partial_sum, 'row', scatter_dimension=0, tiled=True)  86.9 us
    all_gather x3, waiting for transfers between devices, shards(): gathered = lax.all_gather(by_row, 'col', axis=2, tiled=True)  68.6 us
    all_to_all x3, blocking collectives, shards(): lax.all_to_all(by_col, 'row', split_axis=1, concat_axis=0, tiled=True)  67.2 us
    all_gather x1, waiting for transfers between devices, shards(): full_rates = lax.all_gather(rates, 'row', axis=1, tiled=True)  57.2 us
    all_to_all x3, blocking collectives, shards(): lax.all_to_all(spread, 'col', split_axis=2, concat_axis=1, tiled=True)  41.9 us
    unnamed x3, other arithmetic  29 us
  transfers between devices with their start and end apart: 7, of which 5 were waited for; matrix products, arithmetic and copies ran while one was open for 22% of the time, Pallas kernels for 0%

commit v1 on v0

--- a/solution.py
+++ b/solution.py
@@ -18,7 +18,15 @@
         scaled = leak[None, :] * carried
         spread = scaled.reshape(own_rows, local_units // n_col, n_col)
         by_col = lax.all_to_all(spread, "col", split_axis=2, concat_axis=1, tiled=True)
-        by_row = lax.all_to_all(by_col, "row", split_axis=1, concat_axis=0, tiled=True)
+        ways, here = (lax.axis_size("row"), lax.axis_index("row"))
+        width = by_col.shape[1] // ways
+        turned = jnp.roll(by_col, -here * width, axis=1)
+        got = [lax.slice_in_dim(turned, 0, width, axis=1)]
+        for far in range(1, ways):
+            sent = lax.slice_in_dim(turned, far * width, (far + 1) * width, axis=1)
+            got.append(lax.ppermute(sent, "row", [(d, (d + far) % ways) for d in range(ways)]))
+        line = jnp.concatenate(got[::-1], axis=0)
+        by_row = jnp.roll(line, (here + 1) * got[0].shape[0], axis=0)
         gathered = lax.all_gather(by_row, "col", axis=2, tiled=True)
         unit_block = gathered.reshape(gathered.shape[0], gathered.shape[1] * gathered.shape[2])
         rates_now = full_rates[step_back]

time: 642 us -> 611 us (0.952)
  blocking collectives: 109 us -> 26.3 us
  waiting for transfers between devices: 213 us -> 287 us
  other arithmetic: 50.4 us -> 19.8 us
  starting transfers between devices: 1 us -> 20.7 us
  local copies, waits for them, and re-layouts: 33 us -> 20.5 us
    all_to_all x3 -> x0, blocking collectives: 67.2 us -> none  [shards(): lax.all_to_all(by_col, 'row', split_axis=1, concat_axis=0, tiled=True)]
    ppermute x0 -> x9, waiting for transfers between devices: none -> 29 us  [shards(): lax.ppermute(sent, 'row', [(d, (d + far) % ways) for d in range(ways)])]
    unnamed x3 -> x0, other arithmetic: 29 us -> none
    all_gather x1, waiting for transfers between devices: 57.2 us -> 86 us  [shards(): full_rates = lax.all_gather(rates, 'row', axis=1, tiled=True)]
    all_to_all x3 -> x2, blocking collectives: 41.9 us -> 26.3 us  [shards(): lax.all_to_all(spread, 'col', split_axis=2, concat_axis=1, tiled=True)]
    ppermute x0 -> x9, starting transfers between devices: none -> 14.8 us  [shards(): lax.ppermute(sent, 'row', [(d, (d + far) % ways) for d in range(ways)])]
    all_to_all x0 -> x1, waiting for transfers between devices: none -> 9.64 us  [shards(): lax.all_to_all(spread, 'col', split_axis=2, concat_axis=1, tiled=True)]
    unnamed x17 -> x10, local copies, waits for them, and re-layouts: 7.58 us -> 0.02 us
  transfers between devices with their start and end apart: 7 -> 17, of which waited for: 5 -> 12; matrix products, arithmetic and copies ran while one was open for 22% -> 20% of each run, Pallas kernels for 0% -> 0%
where the time goes in v1:
time: 611 us; the launch traced here: 602 us
  waiting for transfers between devices  287 us (47%)
  matrix products  213 us (35%)
  blocking collectives  26.3 us (4%)
  starting transfers between devices  20.7 us (3%)
  local copies, waits for them, and re-layouts  20.5 us (3%)
  other arithmetic  19.8 us (3%)
  between operations  14.5 us (2%)
    dot_general x3, matrix products, shards(): lax.dot_general(unit_block, rates_now, (((0,), (0,)), ((), ())), precisio...  111 us
    dot_general x3, matrix products, shards(): jnp.dot(unit_block, weight, precision=lax.Precision.HIGHEST, preferred_el...  102 us
    reduce_scatter x3, waiting for transfers between devices, shards(): lax.psum_scatter(partial_sum, 'row', scatter_dimension=0, tiled=True)  86.8 us
    all_gather x1, waiting for transfers between devices, shards(): full_rates = lax.all_gather(rates, 'row', axis=1, tiled=True)  86 us
    all_gather x3, waiting for transfers between devices, shards(): gathered = lax.all_gather(by_row, 'col', axis=2, tiled=True)  74.9 us
    ppermute x9, waiting for transfers between devices, shards(): lax.ppermute(sent, 'row', [(d, (d + far) % ways) for d in range(ways)])  29 us
    all_to_all x2, blocking collectives, shards(): lax.all_to_all(spread, 'col', split_axis=2, concat_axis=1, tiled=True)  26.3 us
    all_gather x3, local copies, waits for them, and re-layouts, shards(): gathered = lax.all_gather(by_row, 'col', axis=2, tiled=True)  16.4 us
  transfers between devices with their start and end apart: 17, of which 12 were waited for; matrix products, arithmetic and copies ran while one was open for 20% of the time, Pallas kernels for 0%

profile of v1, /device:TPU:0, one launch (start us, length us, event | category | flops | bytes accessed | tf_op | source)
XLA Modules:
  0.0 602.0 jit_solution(12364587319581738368)
XLA Ops:
  7.2 1.1 broadcast_multiply_fusion.2
  8.6 1.2 copy.17
  9.8 5.2 all-to-all-start
  15.0 9.6 %all-to-all-done = f32[64,256,8]{1,0,2:T(8,128)S(1)} async-done(((f32[64,256,8]{1,0,2:T(8,128)}), f32[64,256,8]{1,0,2:T(8,128)S(1)}, u32[]{:S(2)}, u32[]{:S(2)}) %all-to-all-start) | async-done | bytes 524320 | tf_op jit(solution)/shard_map/all_to_all | solution.py:20
  24.9 1.6 collective-permute-start.2
  26.5 2.6 collective-permute-start.1
  29.1 1.3 collective-permute-start
  30.5 2.2 collective-permute-done.2
  32.7 3.6 collective-permute-done.1
  36.3 1.5 fusion.30
  37.8 38.5 %all-gather.5.cloned.1.call-done = f32[256,512,8]{1,0,2:T(8,128)} async-done(((f32[256,512,1]{1,0,2:T(8,128)}), f32[256,512,8]{1,0,2:T(8,128)}) %all-gather.5.cloned.1.call-update) | async-done | bytes 4194320 | tf_op jit(solution)/shard_map/all_gather | solution.py:30
  76.4 5.5 copy.19
  81.9 33.9 %fusion.9 = f32[256,2048]{1,0:T(8,128)} fusion(f32[4096,2048]{1,0:T(8,128)} %param.8, f32[256,512,8]{0,2,1:T(8,128)} %copy.19), kind=kOutput, calls=%fused_computation.10 | convolution fusion | flops 25769803776 | bytes 39845888 | tf_op jit(solution)/shard_map/dot_general | solution.py:41
  115.8 43.7 %reduce-scatter.4.cloned.1.call-done = f32[64,2048]{1,0:T(8,128)} async-done(((f32[256,2048]{1,0:T(8,128)}), f32[64,2048]{1,0:T(8,128)}) %reduce-scatter.4.cloned.1.call-update) | async-done | bytes 524304 | tf_op jit(solution)/shard_map/reduce_scatter | solution.py:44
  159.5 1.3 broadcast_multiply_fusion.1
  161.2 0.4 copy.21
  161.6 13.2 %all_to_all.54 = f32[64,256,8]{1,0,2:T(8,128)S(1)} all-to-all(f32[64,256,8]{1,0,2:T(8,128)S(1)} %copy.21), channel_id=1, replica_groups=mesh['row'=4,'col'=8] {'col'}, dimensions={2} | all-to-all | bytes 1048576 | tf_op jit(solution)/shard_map/all_to_all | solution.py:20
  174.9 0.7 collective-permute-start.5
  175.7 1.4 collective-permute-start.4
  177.1 2.4 collective-permute-start.3
  179.6 3.6 collective-permute-done.5
  183.2 4.0 collective-permute-done.4
  187.2 1.5 fusion.22
  188.9 36.3 %all-gather.7.cloned.1.call-done = f32[256,512,8]{1,0,2:T(8,128)} async-done(((f32[256,512,1]{1,0,2:T(8,128)}), f32[256,512,8]{1,0,2:T(8,128)}) %all-gather.7.cloned.1.call-update) | async-done | bytes 4194320 | tf_op jit(solution)/shard_map/all_gather | solution.py:30
  225.3 5.5 copy.23
  230.7 33.8 %fusion.5 = f32[256,2048]{1,0:T(8,128)} fusion(f32[4096,2048]{1,0:T(8,128)} %param.8, f32[256,512,8]{0,2,1:T(8,128)} %copy.23), kind=kOutput, calls=%fused_computation.6 | convolution fusion | flops 25769803776 | bytes 39845888 | tf_op jit(solution)/shard_map/dot_general | solution.py:41
  264.7 0.5 all-gather.11.cloned.1.call-update
  265.3 43.2 %reduce-scatter.6.cloned.1.call-done = f32[64,2048]{1,0:T(8,128)} async-done(((f32[256,2048]{1,0:T(8,128)}), f32[64,2048]{1,0:T(8,128)}) %reduce-scatter.6.cloned.1.call-update) | async-done | bytes 524304 | tf_op jit(solution)/shard_map/reduce_scatter | solution.py:44
  308.4 2.0 broadcast_multiply_fusion
  310.8 0.4 copy.25
  311.2 13.1 %all_to_all.55 = f32[64,256,8]{1,0,2:T(8,128)S(1)} all-to-all(f32[64,256,8]{1,0,2:T(8,128)S(1)} %copy.25), channel_id=1, replica_groups=mesh['row'=4,'col'=8] {'col'}, dimensions={2} | all-to-all | bytes 1048576 | tf_op jit(solution)/shard_map/all_to_all | solution.py:20
  324.5 0.7 collective-permute-start.8
  325.3 1.5 collective-permute-start.7
  326.7 2.4 collective-permute-start.6
  329.2 6.4 %collective-permute-done.8 = f32[64,512,1]{1,0,2:T(8,128)S(1)} collective-permute-done((f32[64,512,1]{1,0,2:T(8,128)S(1)}, f32[64,512,1]{1,0,2:T(8,128)S(1)}, u32[]{:S(2)}, u32[]{:S(2)}) %collective-permute-start.8) | collective-permute-done | bytes 131104 | tf_op jit(solution)/shard_map/ppermute | solution.py:27
  335.6 9.2 %collective-permute-done.7 = f32[64,512,1]{1,0,2:T(8,128)S(1)} collective-permute-done((f32[64,512,1]{1,0,2:T(8,128)S(1)}, f32[64,512,1]{1,0,2:T(8,128)S(1)}, u32[]{:S(2)}, u32[]{:S(2)}) %collective-permute-start.7) | collective-permute-done | bytes 131104 | tf_op jit(solution)/shard_map/ppermute | solution.py:27
  344.8 1.5 fusion.14
  346.6 2.6 reduce_sum.29
  349.5 86.0 %all-gather.11.cloned.1.call-done = f32[3,256,2048]{2,1,0:T(8,128)} async-done(((f32[3,64,2048]{2,1,0:T(8,128)}), f32[3,256,2048]{2,1,0:T(8,128)}) %all-gather.11.cloned.1.call-update) | async-done | bytes 6291472 | tf_op jit(solution)/shard_map/all_gather | solution.py:13
  435.5 32.4 %fusion.7 = f32[4096,2048]{1,0:T(8,128)} fusion(f32[256,512,8]{0,2,1:T(8,128)} %copy.19, f32[3,256,2048]{2,1,0:T(8,128)} %all-gather.11.cloned.1.call-done), kind=kOutput, calls=%fused_computation.8 | convolution fusion | flops 25769803776 | bytes 39845888 | tf_op jit(solution)/shard_map/dot_general | solution.py:34
  467.9 2.7 reduce_sum.28
  470.9 32.5 %fusion.3 = f32[4096,2048]{1,0:T(8,128)} fusion(f32[256,512,8]{0,2,1:T(8,128)} %copy.23, f32[3,256,2048]{2,1,0:T(8,128)} %all-gather.11.cloned.1.call-done), kind=kOutput, calls=%fused_computation.4 | convolution fusion | flops 25769803776 | bytes 39845888 | tf_op jit(solution)/shard_map/dot_general | solution.py:34
  503.4 2.6 reduce_sum.27
  506.3 5.5 copy.27
  511.7 34.2 %fusion.1 = f32[256,2048]{1,0:T(8,128)} fusion(f32[4096,2048]{1,0:T(8,128)} %param.8, f32[256,512,8]{0,2,1:T(8,128)} %copy.27), kind=kOutput, calls=%fused_computation.2 | convolution fusion | flops 25769803776 | bytes 39845888 | tf_op jit(solution)/shard_map/dot_general | solution.py:41
  546.0 0.7 pad_maximum_fusion
  546.7 46.3 %add_add_fusion = f32[4096,2048]{1,0:T(8,128)} fusion(f32[4096,2048]{1,0:T(8,128)} %fusion.7, f32[4096,2048]{1,0:T(8,128)} %fusion.3, f32[256,512,8]{0,2,1:T(8,128)} %copy.27, f32[3,256,2048]{2,1,0:T(8,128)} %all-gather.11.cloned.1.call-done), kind=kOutput, calls=%fused_computation | convolution fusion | flops 25786580992 | bytes 106954752 | tf_op jit(solution)/shard_map/dot_general | solution.py:34
  593.0 1.9 fusion.35
  (47 shorter events, 3.2 us)
Async XLA Ops:
  9.8 14.9 %all-to-all-start = ((f32[64,256,8]{1,0,2:T(8,128)}), f32[64,256,8]{1,0,2:T(8,128)S(1)}, u32[]{:S(2)}, u32[]{:S(2)}) async-start(f32[64,256,8]{1,0,2:T(8,128)} %copy.17), calls=%async_computation | async-start | bytes 1048576 | tf_op jit(solution)/shard_map/all_to_all | solution.py:20
  15.0 61.4 %all-gather.5.cloned.1.call-start = ((), (), s32[]{:S(2)}) async-start(), calls=%async_computation.6 | async-start | bytes 4718592 | tf_op jit(solution)/shard_map/all_gather | solution.py:30
  24.9 7.8 %collective-permute-start.2 = (f32[64,512,1]{1,0,2:T(8,128)S(1)}, f32[64,512,1]{1,0,2:T(8,128)S(1)}, u32[]{:S(2)}, u32[]{:S(2)}) collective-permute-start(f32[64,512,1]{1,0,2:T(8,128)S(1)} %get-tuple-element.16), channel_id=1, source_target_pairs={{0,8},{8,16},{16,24},{24,0},{1,9},{9,17},{17,25},{25,1},{2,10},{10... | collective-permute-start | bytes 393224 | tf_op jit(solution)/shard_map/ppermute | solution.py:27
  26.5 9.7 %collective-permute-start.1 = (f32[64,512,1]{1,0,2:T(8,128)S(1)}, f32[64,512,1]{1,0,2:T(8,128)S(1)}, u32[]{:S(2)}, u32[]{:S(2)}) collective-permute-start(f32[64,512,1]{1,0,2:T(8,128)S(1)} %get-tuple-element.17), channel_id=1, source_target_pairs={{0,16},{8,24},{16,0},{24,8},{1,17},{9,25},{17,1},{25,9},{2,18},{10... | collective-permute-start | bytes 393224 | tf_op jit(solution)/shard_map/ppermute | solution.py:27
  29.1 7.2 %collective-permute-start = (f32[64,512,1]{1,0,2:T(8,128)S(1)}, f32[64,512,1]{1,0,2:T(8,128)S(1)}, u32[]{:S(2)}, u32[]{:S(2)}) collective-permute-start(f32[64,512,1]{1,0,2:T(8,128)S(1)} %get-tuple-element.18), channel_id=1, source_target_pairs={{0,24},{8,0},{16,8},{24,16},{1,25},{9,1},{17,9},{25,17},{2,26},{10... | collective-permute-start | bytes 393224 | tf_op jit(solution)/shard_map/ppermute | solution.py:27
  37.8 121.7 %reduce-scatter.4.cloned.1.call-start = ((), (), s32[]{:S(2)}) async-start(), calls=%async_computation.7 | async-start | bytes 2621440 | tf_op jit(solution)/shard_map/reduce_scatter | solution.py:44
  81.9 33.9 %copy-start.4 = (f32[2048]{0:T(1024)S(1)}, f32[2048]{0:T(1024)}, u32[]{:S(2)}) copy-start(f32[2048]{0:T(1024)} %param.9) | copy-start | bytes 24580
  81.9 77.6 %copy-start.1 = (f32[64,2048]{1,0:T(8,128)S(1)}, f32[64,2048]{1,0:T(8,128)}, u32[]{:S(2)}) copy-start(f32[64,2048]{1,0:T(8,128)} %param.11) | copy-start | bytes 1572868
  115.8 109.5 %all-gather.7.cloned.1.call-start = ((), (), s32[]{:S(2)}) async-start(), calls=%async_computation.8 | async-start | bytes 4718592 | tf_op jit(solution)/shard_map/all_gather | solution.py:30
  174.9 8.2 %collective-permute-start.5 = (f32[64,512,1]{1,0,2:T(8,128)S(1)}, f32[64,512,1]{1,0,2:T(8,128)S(1)}, u32[]{:S(2)}, u32[]{:S(2)}) collective-permute-start(f32[64,512,1]{1,0,2:T(8,128)S(1)} %get-tuple-element.12), channel_id=1, source_target_pairs={{0,8},{8,16},{16,24},{24,0},{1,9},{9,17},{17,25},{25,1},{2,10},{10... | collective-permute-start | bytes 393224 | tf_op jit(solution)/shard_map/ppermute | solution.py:27
  175.7 11.5 %collective-permute-start.4 = (f32[64,512,1]{1,0,2:T(8,128)S(1)}, f32[64,512,1]{1,0,2:T(8,128)S(1)}, u32[]{:S(2)}, u32[]{:S(2)}) collective-permute-start(f32[64,512,1]{1,0,2:T(8,128)S(1)} %get-tuple-element.13), channel_id=1, source_target_pairs={{0,16},{8,24},{16,0},{24,8},{1,17},{9,25},{17,1},{25,9},{2,18},{10... | collective-permute-start | bytes 393224 | tf_op jit(solution)/shard_map/ppermute | solution.py:27
  177.1 10.1 %collective-permute-start.3 = (f32[64,512,1]{1,0,2:T(8,128)S(1)}, f32[64,512,1]{1,0,2:T(8,128)S(1)}, u32[]{:S(2)}, u32[]{:S(2)}) collective-permute-start(f32[64,512,1]{1,0,2:T(8,128)S(1)} %get-tuple-element.14), channel_id=1, source_target_pairs={{0,24},{8,0},{16,8},{24,16},{1,25},{9,1},{17,9},{25,17},{2,26},{10... | collective-permute-start | bytes 393224 | tf_op jit(solution)/shard_map/ppermute | solution.py:27
  188.7 119.7 %reduce-scatter.6.cloned.1.call-start = ((), (), s32[]{:S(2)}) async-start(), calls=%async_computation.9 | async-start | bytes 2621440 | tf_op jit(solution)/shard_map/reduce_scatter | solution.py:44
  230.7 77.7 %copy-start.3 = (f32[64,2048]{1,0:T(8,128)S(1)}, f32[64,2048]{1,0:T(8,128)}, u32[]{:S(2)}) copy-start(f32[64,2048]{1,0:T(8,128)} %reduce-scatter.4.cloned.1.call-done) | copy-start | bytes 1572868
  264.6 43.8 %copy-start = (f32[3,64,2048]{2,1,0:T(8,128)S(1)}, f32[3,64,2048]{2,1,0:T(8,128)}, u32[]{:S(2)}) copy-start(f32[3,64,2048]{2,1,0:T(8,128)} %param.10) | copy-start | bytes 4718596
  264.6 170.9 %all-gather.11.cloned.1.call-start = ((), (), s32[]{:S(2)}) async-start(), calls=%async_computation.12 | async-start | bytes 7864320 | tf_op jit(solution)/shard_map/all_gather | solution.py:13
  265.2 238.1 %all-gather.9.cloned.1.call-start = ((), (), s32[]{:S(2)}) async-start(), calls=%async_computation.10 | async-start | bytes 4718592 | tf_op jit(solution)/shard_map/all_gather | solution.py:30
  324.5 11.0 %collective-permute-start.8 = (f32[64,512,1]{1,0,2:T(8,128)S(1)}, f32[64,512,1]{1,0,2:T(8,128)S(1)}, u32[]{:S(2)}, u32[]{:S(2)}) collective-permute-start(f32[64,512,1]{1,0,2:T(8,128)S(1)} %get-tuple-element.8), channel_id=1, source_target_pairs={{0,8},{8,16},{16,24},{24,0},{1,9},{9,17},{17,25},{25,1},{2,10},{10... | collective-permute-start | bytes 393224 | tf_op jit(solution)/shard_map/ppermute | solution.py:27
  325.3 19.5 %collective-permute-start.7 = (f32[64,512,1]{1,0,2:T(8,128)S(1)}, f32[64,512,1]{1,0,2:T(8,128)S(1)}, u32[]{:S(2)}, u32[]{:S(2)}) collective-permute-start(f32[64,512,1]{1,0,2:T(8,128)S(1)} %get-tuple-element.9), channel_id=1, source_target_pairs={{0,16},{8,24},{16,0},{24,8},{1,17},{9,25},{17,1},{25,9},{2,18},{10... | collective-permute-start | bytes 393224 | tf_op jit(solution)/shard_map/ppermute | solution.py:27
  326.7 18.0 %collective-permute-start.6 = (f32[64,512,1]{1,0,2:T(8,128)S(1)}, f32[64,512,1]{1,0,2:T(8,128)S(1)}, u32[]{:S(2)}, u32[]{:S(2)}) collective-permute-start(f32[64,512,1]{1,0,2:T(8,128)S(1)} %get-tuple-element.10), channel_id=1, source_target_pairs={{0,24},{8,0},{16,8},{24,16},{1,25},{9,1},{17,9},{25,17},{2,26},{10... | collective-permute-start | bytes 393224 | tf_op jit(solution)/shard_map/ppermute | solution.py:27
  346.3 246.7 %reduce-scatter.8.cloned.1.call-start = ((), (), s32[]{:S(2)}) async-start(), calls=%async_computation.11 | async-start | bytes 2621440 | tf_op jit(solution)/shard_map/reduce_scatter | solution.py:44
  546.7 46.3 %copy-start.2 = (f32[64,2048]{1,0:T(8,128)S(1)}, f32[64,2048]{1,0:T(8,128)}, u32[]{:S(2)}) copy-start(f32[64,2048]{1,0:T(8,128)} %get-tuple-element.6) | copy-start | bytes 1572868
Sparse Core Ops, SparseCore 0:
  37.9 38.3 all-gather.4
  115.9 43.5 reduce-scatter.3
  188.8 36.4 all-gather.6
  264.7 43.6 reduce-scatter.5
  309.8 125.6 all-gather.10
  437.2 34.7 all-gather.8
  546.1 41.7 reduce-scatter.7
